TPU v7x, 128 devices: a whole 4x4x4 slice. The times are simulated.
128 devices in a mesh: walker: 16 (over x, y_hi, core), prow: 2 (over y_lo), pcol: 4 (over z).
Axes of the slice: x: 4, y: 4 (y_hi: 2, y_lo: 2; y = y_hi * 2 + y_lo), z: 4, core: 2. Of those that a mesh axis runs over, the one named last changes fastest.
Arguments:
- o_rows: bfloat16 [32768, 2048], P('walker', ('prow', 'pcol')), may hold values from -21 to 21
- o_cols: bfloat16 [32768, 4096], P('walker', ('pcol', 'prow')), may hold values from -48 to 48
- grad_energy: bfloat16 [32768, 4096], P('walker', ('pcol', 'prow')), may hold values from -8 to 8
- energy: float32 [32768], P('walker'), may hold values from -5 to 1
Outputs:
- hamil: float32 [2048, 4096], P(('prow', 'walker'), 'pcol')
- correlation: float32 [2048, 4096], P(('prow', 'walker'), 'pcol')
All inputs are finite; a program needn't handle non-finite values.
Results may differ from a plain program's by a relative error of at most 0.008.
Values may be sent and summed in bfloat16 or wider, within the bound.
A program may use at most 128 MiB of HBM per device.

v0:
```python
import jax
import jax.numpy as jnp
from jax import lax
from jax.sharding import PartitionSpec as P


def column_sums(values):
    return jnp.sum(values.astype(jnp.float32), axis=0)


def tile_product(row_tile, right_tile):
    return lax.dot_general(
        row_tile, right_tile, (((0,), (0,)), ((), ())), preferred_element_type=jnp.float32
    )


def per_device(o_rows, o_cols, grad_energy, energy):
    count = energy.shape[0] * lax.axis_size("walker")
    row_total, col_total = lax.psum((column_sums(o_rows), column_sums(o_cols)), "walker")
    row_shard = (o_rows - row_total / count).astype(jnp.bfloat16)
    col_shard = (o_cols - col_total / count).astype(jnp.bfloat16)
    row_tile = lax.all_gather(row_shard, "pcol", axis=1, tiled=True)
    col_tile, grad_tile = (
        lax.all_gather(col_shard, "prow", axis=1, tiled=True),
        lax.all_gather(grad_energy, "prow", axis=1, tiled=True),
    )
    weighted = (energy[:, None] * col_tile + grad_tile).astype(jnp.bfloat16)
    paired = jnp.concatenate((col_tile, weighted), axis=1)
    summed = lax.psum_scatter(
        tile_product(row_tile, paired), "walker", scatter_dimension=0, tiled=True
    )
    width = col_tile.shape[1]
    correlation = summed[:, :width]
    hamil = summed[:, width:]
    return (hamil / count, correlation / count)


def solution(mesh):
    in_specs = (
        P("walker", ("prow", "pcol")),
        P("walker", ("pcol", "prow")),
        P("walker", ("pcol", "prow")),
        P("walker"),
    )
    out_specs = (P(("prow", "walker"), "pcol"), P(("prow", "walker"), "pcol"))
    return jax.shard_map(
        per_device, mesh=mesh, in_specs=in_specs, out_specs=out_specs, check_vma=False
    )
```

profile of v0, /device:TPU:4, one launch (start us, length us, event | category | flops | bytes accessed | tf_op | source)
XLA Modules:
  0.0 313.1 jit_solution(17419922395982080322)
XLA Ops:
  7.2 0.0 copy-start
  7.2 0.0 all-gather.8.cloned.1.call-start
  7.2 0.7 all-gather.8.cloned.1.call-update
  7.9 0.0 all-gather.6.cloned.1.call-start
  8.0 1.5 convert_reduce_fusion.1
  9.5 0.0 copy-done
  9.5 0.0 copy-start.1
  9.5 0.3 convert_reduce_fusion
  9.8 31.3 %all-reduce = (f32[256]{0:T(256)S(1)}, f32[512]{0:T(512)S(1)}) all-reduce(f32[256]{0:T(256)S(1)} %convert_reduce_fusion.1, f32[512]{0:T(512)S(1)} %convert_reduce_fusion), channel_id=1, replica_groups=mesh['walker'=16,'prow'=2,'pcol'=4] {'walker'}, use_global_device_ids=true, to_apply=%region_1.0 | all-reduce | flops 768 | bytes 6144 | tf_op jit(solution)/shard_map/psum | solution.py:19
  41.2 0.0 copy-start.2
  41.2 1.8 fusion.4
  42.9 0.0 all-gather.6.cloned.1.call-update
  43.0 0.0 all-gather.4.cloned.1.call-start
  43.0 0.0 copy-done.1
  43.0 1.2 fusion.5
  44.3 0.0 all-gather.4.cloned.1.call-update
  44.3 0.0 reduce-scatter.2.cloned.1.call-start
  44.3 27.3 %all-gather.8.cloned.1.call-done = bf16[2048,1024]{1,0:T(8,128)(2,1)} async-done(((bf16[2048,512]{1,0:T(8,128)(2,1)}), bf16[2048,1024]{1,0:T(8,128)(2,1)}) %all-gather.8.cloned.1.call-update) | async-done | bytes 4194320 | tf_op jit(solution)/shard_map/all_gather | solution.py:25
  71.6 61.9 %all-gather.6.cloned.1.call-done = bf16[2048,1024]{1,0:T(8,128)(2,1)} async-done(((bf16[2048,512]{1,0:T(8,128)(2,1)}), bf16[2048,1024]{1,0:T(8,128)(2,1)}) %all-gather.6.cloned.1.call-update) | async-done | bytes 4194320 | tf_op jit(solution)/shard_map/all_gather | solution.py:24
  133.5 0.0 copy-done.2
  133.5 5.4 %add_convert_fusion = bf16[2048,1024]{1,0:T(8,128)(2,1)} fusion(bf16[2048,1024]{1,0:T(8,128)(2,1)} %all-gather.8.cloned.1.call-done, bf16[2048,1024]{1,0:T(8,128)(2,1)} %all-gather.6.cloned.1.call-done, f32[2048]{0:T(1024)S(1)} %copy-done.2), kind=kLoop, calls=%fused_computation.4 | loop fusion | flops 10485760 | bytes 12591104 | tf_op jit(solution)/shard_map/convert_element_type | solution.py:27
  139.0 48.8 %all-gather.4.cloned.1.call-done = bf16[2048,1024]{1,0:T(8,128)(2,1)} async-done(((bf16[2048,256]{1,0:T(8,128)(2,1)}), bf16[2048,1024]{1,0:T(8,128)(2,1)}) %all-gather.4.cloned.1.call-update) | async-done | bytes 4194320 | tf_op jit(solution)/shard_map/all_gather | solution.py:22
  187.8 15.2 %fusion = f32[1024,2048]{1,0:T(8,128)} fusion(bf16[2048,1024]{1,0:T(8,128)(2,1)} %all-gather.4.cloned.1.call-done, bf16[2048,1024]{1,0:T(8,128)(2,1)} %add_convert_fusion, bf16[2048,1024]{1,0:T(8,128)(2,1)} %all-gather.6.cloned.1.call-done), kind=kOutput, calls=%fused_computation | convolution fusion | flops 8606711808 | bytes 20971520 | tf_op jit(solution)/shard_map/dot_general | solution.py:12
  202.9 0.0 reduce-scatter.2.cloned.1.call-update
  203.0 101.8 %reduce-scatter.2.cloned.1.call-done = f32[64,2048]{1,0:T(8,128)} async-done(((f32[1024,2048]{1,0:T(8,128)}), f32[64,2048]{1,0:T(8,128)}) %reduce-scatter.2.cloned.1.call-update) | async-done | bytes 524304 | tf_op jit(solution)/shard_map/reduce_scatter | solution.py:29
  304.7 1.9 slice_multiply_fusion
  (2 shorter events, 0.0 us)
Async XLA Ops:
  7.2 2.3 copy-start
  7.2 64.4 %all-gather.8.cloned.1.call-start = ((), (), s32[]{:S(2)}) async-start(), calls=%async_computation.3 | async-start | bytes 6291456 | tf_op jit(solution)/shard_map/all_gather | solution.py:25
  7.9 125.6 %all-gather.6.cloned.1.call-start = ((), (), s32[]{:S(2)}) async-start(), calls=%async_computation.2 | async-start | bytes 6291456 | tf_op jit(solution)/shard_map/all_gather | solution.py:24
  9.5 33.6 %copy-start.1 = (bf16[2048,256]{1,0:T(8,128)(2,1)S(1)}, bf16[2048,256]{1,0:T(8,128)(2,1)}, u32[]{:S(2)}) copy-start(bf16[2048,256]{1,0:T(8,128)(2,1)} %param.4) | copy-start | bytes 3145732
  41.2 92.3 %copy-start.2 = (f32[2048]{0:T(1024)S(1)}, f32[2048]{0:T(1024)}, u32[]{:S(2)}) copy-start(f32[2048]{0:T(1024)} %param.7) | copy-start | bytes 24580
  43.0 144.8 %all-gather.4.cloned.1.call-start = ((), (), s32[]{:S(2)}) async-start(), calls=%async_computation.1 | async-start | bytes 5242880 | tf_op jit(solution)/shard_map/all_gather | solution.py:22
  44.3 260.4 %reduce-scatter.2.cloned.1.call-start = ((), (), s32[]{:S(2)}) async-start(), calls=%async_computation.4 | async-start | bytes 8912896 | tf_op jit(solution)/shard_map/reduce_scatter | solution.py:29
Sparse Core Ops, SparseCore 0:
  9.6 61.9 all-gather.7
  73.3 60.2 all-gather.5
  135.2 52.5 all-gather.3
  203.1 101.5 reduce-scatter.1
where the time goes:
time: 315 us; the launch traced here: 313 us
  waiting for transfers between devices  240 us (76%)
  blocking collectives  31.3 us (10%)
  matrix products  15.2 us (5%)
  between operations  13.8 us (4%)
  other arithmetic  12.2 us (4%)
    reduce_scatter x1, waiting for transfers between devices, per_device(): lax.psum_scatter(tile_product(row_tile, paired), 'walker', scatter_dimens...  102 us
    all_gather x1, waiting for transfers between devices, per_device(): lax.all_gather(col_shard, 'prow', axis=1, tiled=True)  61.9 us
    all_gather x1, waiting for transfers between devices, per_device(): row_tile = lax.all_gather(row_shard, 'pcol', axis=1, tiled=True)  48.8 us
    psum x1, blocking collectives, per_device(): lax.psum((column_sums(o_rows), column_sums(o_cols)), 'walker')  31.3 us
    all_gather x1, waiting for transfers between devices, per_device(): lax.all_gather(grad_energy, 'prow', axis=1, tiled=True)  27.3 us
    dot_general x1, matrix products, tile_product(): lax.dot_general(row_tile, right_tile, (((0,), (0,)), ((), ())), preferred...  15.2 us
  transfers between devices with their start and end apart: 4, of which 4 were waited for; matrix products, arithmetic and copies ran while one was open for 3% of the time, Pallas kernels for 0%

commit v1 on v0

v1 whole, which is shorter than its diff:
```python
import functools

import jax
import jax.numpy as jnp
from jax import lax
from jax.experimental import pallas as pl
from jax.experimental.pallas import tpu as pltpu
from jax.sharding import PartitionSpec as P

MESH = pl.DeviceIdType.MESH
F32 = jnp.float32
BF16 = jnp.bfloat16

PIECE = 512


def kernel(total, o_hbm, c_hbm, g_hbm, e_hbm, ham_ref, cor_ref,
           rows, cols, grads, en, rhs, pacc, stat, stat_x, rmean,
           core_out, core_in, x_out, x_in, x_acc, y_out, y_in, y_keep,
           load_sem, rs_send, rs_recv, st_send, st_recv, rm_send, rm_recv,
           c_send, c_recv, x_send, x_recv, y_send, y_recv):
    w = lax.axis_index("walker")
    p = lax.axis_index("prow")
    q = lax.axis_index("pcol")
    x, yh, c = w // 4, (w // 2) % 2, w % 2

    def walker(xx, yy, cc):
        return xx * 4 + yy * 2 + cc

    partner = (walker(x, yh, 1 - c), p, q)
    xs = [(walker((x + k) % 4, yh, c), p, q) for k in (1, 2, 3)]
    far = (walker(x, 1 - yh, c), p, q)
    near = (w, 1 - p, q)
    diag = (walker(x, 1 - yh, c), 1 - p, q)
    up = (w, p, (q + 1) % 4)
    down = (w, p, (q + 3) % 4)
    peers = [partner, *xs, far, near, diag, up, down]

    loads = [
        pltpu.make_async_copy(o_hbm, rows.at[0], load_sem.at[0]),
        pltpu.make_async_copy(c_hbm, cols, load_sem.at[1]),
        pltpu.make_async_copy(e_hbm, en, load_sem.at[2]),
        pltpu.make_async_copy(g_hbm, grads, load_sem.at[3]),
    ]
    for load in loads:
        load.start()

    barrier = pltpu.get_barrier_semaphore()
    for peer in peers:
        pl.semaphore_signal(barrier, inc=1, device_id=peer, device_id_type=MESH)
    pl.semaphore_wait(barrier, len(peers))

    started = []

    def start(src, dst, send, recv, device):
        copy = pltpu.make_async_remote_copy(
            src_ref=src, dst_ref=dst, send_sem=send, recv_sem=recv,
            device_id=device, device_id_type=MESH)
        copy.start()
        started.append(copy)

    def arrived(dst, recv):
        pltpu.make_async_remote_copy(
            src_ref=dst, dst_ref=dst, send_sem=recv, recv_sem=recv,
            device_id=near, device_id_type=MESH).wait_recv()

    counter = [0]

    def piece_of(slot, i):
        if slot == 0:
            return o_hbm.at[pl.ds(i * PIECE, PIECE)]
        return rows.at[slot, pl.ds(i * PIECE, PIECE)]

    def send_piece(way, dy, dz, i):
        device, ty, tz = {
            "up": (up, dy, (dz + 3) % 4),
            "down": (down, dy, (dz + 1) % 4),
            "across": (near, 1 - dy, dz),
        }[way]
        target = ty * 4 + tz
        n = counter[0]
        counter[0] += 1
        start(piece_of(dy * 4 + dz, i), rows.at[target, pl.ds(i * PIECE, PIECE)],
              rs_send.at[n], rs_recv.at[target, i], device)

    def piece_in(dy, dz, i):
        slot = dy * 4 + dz
        arrived(rows.at[slot, pl.ds(i * PIECE, PIECE)], rs_recv.at[slot, i])

    send_piece("up", 0, 0, 0)
    send_piece("down", 0, 0, 1)
    send_piece("across", 0, 0, 2)

    loads[0].wait()
    loads[1].wait()

    def sums(i, carry):
        a, b = carry
        at = pl.ds(pl.multiple_of(i * 128, 128), 128)
        a = a + jnp.sum(rows[0, at, :].astype(F32).reshape(16, 8, 256), axis=0)
        b = b + jnp.sum(cols[at, :].astype(F32).reshape(16, 8, 512), axis=0)
        return a, b

    a, b = lax.fori_loop(0, 16, sums, (jnp.zeros((8, 256), F32), jnp.zeros((8, 512), F32)))
    stat[0, :, 0:256] = a
    stat[0, :, 256:768] = b
    start(stat.at[0], stat.at[1], st_send.at[0], st_recv.at[0], partner)
    arrived(stat.at[1], st_recv.at[0])
    stat[2] = stat[0] + stat[1]
    for k in range(3):
        start(stat.at[2], stat_x.at[k], st_send.at[1 + k], st_recv.at[1 + k], xs[k])
    for k in range(3):
        arrived(stat_x.at[k], st_recv.at[1 + k])
    stat[3] = (stat[2] + stat_x[1]) + (stat_x[0] + stat_x[2])
    start(stat.at[3], stat.at[4], st_send.at[4], st_recv.at[4], far)
    send_piece("up", 0, 0, 1)
    send_piece("down", 0, 0, 0)
    send_piece("across", 0, 0, 3)
    arrived(stat.at[4], st_recv.at[4])
    mean = jnp.sum(stat[3] + stat[4], axis=0, keepdims=True) / total
    rmean[0, 0] = jnp.broadcast_to(mean[:, 0:256], (8, 256))
    start(rmean.at[0, 0], rmean.at[0, 1], rm_send.at[0], rm_recv.at[0], near)
    send_piece("up", 0, 0, 2)
    send_piece("down", 0, 0, 3)
    send_piece("across", 0, 0, 0)

    loads[2].wait()
    loads[3].wait()
    col_mean = mean[:, 256:768]

    def right(i, carry):
        at = pl.ds(pl.multiple_of(i * 128, 128), 128)
        d = (cols[at, :].astype(F32) - col_mean).astype(BF16)
        e = jnp.broadcast_to(en[pl.ds(i, 1), :], (128, 128)).T
        e = jnp.concatenate([e, e, e, e], axis=1)
        rhs[at, 0:512] = d
        rhs[at, 512:1024] = (e * d.astype(F32) + grads[at, :].astype(F32)).astype(BF16)
        return carry

    lax.fori_loop(0, 16, right, 0)

    def multiply(dy, dz, order=0, wait=False):
        slot = dy * 4 + dz
        bank = slot % 2
        m = rmean[dz, dy, 0:1, :]
        pacc[bank] = jnp.zeros((256, 1024), F32)

        def step(i, carry):
            i = lax.rem(i + order, 4)
            at = pl.ds(pl.multiple_of(i * PIECE, PIECE), PIECE)
            if wait:
                arrived(rows.at[slot, at], rs_recv.at[slot, i])
            d = (rows[slot, at, :].astype(F32) - m).astype(BF16).T
            for h in range(2):
                cut = slice(h * 512, h * 512 + 512)
                pacc[bank, :, cut] += jnp.dot(d, rhs[at, cut], preferred_element_type=F32)
            return carry

        lax.fori_loop(0, 4, step, 0)
        for r in range(2):
            core_out[slot, r * 64:r * 64 + 64, :] = pacc[
                bank, pl.ds(pl.multiple_of(r * 128 + (1 - c) * 64, 64), 64), :].astype(BF16)
        start(core_out.at[slot], core_in.at[slot], c_send.at[slot], c_recv.at[slot], partner)

    def x_copy(dy, dz):
        slot = dy * 4 + dz
        owner = (q + dz) % 4
        k = (x - owner + 3) % 4
        return pltpu.make_async_remote_copy(
            src_ref=x_out.at[slot], dst_ref=x_in.at[dy, k],
            send_sem=x_send.at[slot], recv_sem=x_recv.at[dy, k],
            device_id=(walker(owner, yh, c), p, q), device_id_type=MESH)

    def combine(dy, dz):
        slot = dy * 4 + dz
        bank = slot % 2
        owner = (q + dz) % 4
        arrived(core_in.at[slot], c_recv.at[slot])
        parts = [
            pacc[bank, pl.ds(pl.multiple_of(r * 128 + c * 64, 64), 64), :]
            + core_in[slot, r * 64:r * 64 + 64, :].astype(F32)
            for r in range(2)
        ]

        @pl.when(owner == x)
        def _():
            for r in range(2):
                x_acc[dy, r * 64:r * 64 + 64, :] = parts[r]

        @pl.when(owner != x)
        def _():
            for r in range(2):
                x_out[slot, r * 64:r * 64 + 64, :] = parts[r].astype(BF16)
            x_copy(dy, dz).start()

    def x_total(dy, half):
        at = pl.ds(pl.multiple_of(half * 64, 64), 64)
        got = [x_in[dy, k, at, :].astype(F32) for k in range(3)]
        return (x_acc[dy, at, :] + got[1]) + (got[0] + got[2])

    multiply(0, 0)
    arrived(rmean.at[0, 1], rm_recv.at[0])
    start(rmean.at[0], rmean.at[3], rm_send.at[1], rm_recv.at[1], up)
    start(rmean.at[0], rmean.at[1], rm_send.at[2], rm_recv.at[2], down)
    send_piece("up", 0, 0, 3)
    send_piece("down", 0, 0, 2)
    send_piece("across", 0, 0, 1)
    combine(0, 0)

    piece_in(0, 3, 0)
    send_piece("up", 0, 3, 0)
    send_piece("across", 0, 3, 0)
    piece_in(0, 1, 1)
    send_piece("down", 0, 1, 1)
    send_piece("across", 0, 1, 1)
    piece_in(0, 3, 1)
    send_piece("across", 0, 3, 1)
    piece_in(0, 1, 0)
    send_piece("across", 0, 1, 0)
    arrived(rmean.at[3], rm_recv.at[1])
    start(rmean.at[3], rmean.at[2], rm_send.at[3], rm_recv.at[3], up)
    arrived(rmean.at[1], rm_recv.at[2])
    piece_in(0, 3, 2)
    send_piece("up", 0, 3, 2)
    piece_in(0, 1, 3)
    send_piece("down", 0, 1, 3)
    piece_in(1, 0, 2)
    send_piece("up", 1, 0, 2)
    piece_in(1, 0, 3)
    send_piece("down", 1, 0, 3)
    send_piece("up", 1, 0, 3)
    send_piece("down", 1, 0, 2)

    piece_in(1, 0, 0)
    piece_in(1, 0, 1)
    multiply(1, 0)
    piece_in(0, 3, 3)
    multiply(0, 3)
    combine(1, 0)
    combine(0, 3)
    piece_in(0, 1, 2)
    multiply(0, 1)
    piece_in(0, 2, 0)
    send_piece("across", 0, 2, 0)
    piece_in(0, 2, 1)
    send_piece("across", 0, 2, 1)
    combine(0, 1)
    arrived(rmean.at[2], rm_recv.at[3])
    piece_in(0, 2, 2)
    piece_in(0, 2, 3)
    multiply(0, 2)
    combine(0, 2)

    piece_in(1, 3, 2)
    send_piece("up", 1, 3, 2)
    piece_in(1, 1, 3)
    send_piece("down", 1, 1, 3)
    piece_in(1, 3, 0)
    piece_in(1, 3, 1)
    piece_in(1, 3, 3)
    multiply(1, 3)
    combine(1, 3)
    piece_in(1, 1, 0)
    piece_in(1, 1, 1)
    piece_in(1, 1, 2)
    multiply(1, 1)
    combine(1, 1)

    for k in range(3):
        arrived(x_in.at[0, k], x_recv.at[0, k])
    y_keep[...] = x_total(0, yh)
    y_out[0] = x_total(0, 1 - yh).astype(BF16)
    start(y_out.at[0], y_in.at[0], y_send.at[0], y_recv.at[0], far)

    multiply(1, 2, order=2, wait=True)
    combine(1, 2)

    for k in range(3):
        arrived(x_in.at[1, k], x_recv.at[1, k])
    y_out[1] = x_total(1, yh).astype(BF16)
    start(y_out.at[1], y_in.at[1], y_send.at[1], y_recv.at[1], near)
    y_out[2] = x_total(1, 1 - yh).astype(BF16)
    start(y_out.at[2], y_in.at[2], y_send.at[2], y_recv.at[2], diag)

    scale = 1.0 / total
    mine = pl.ds(pl.multiple_of(p * 512, 512), 512)
    other = pl.ds(pl.multiple_of((1 - p) * 512, 512), 512)
    arrived(y_in.at[0], y_recv.at[0])
    for ref, cut in ((cor_ref, slice(0, 512)), (ham_ref, slice(512, 1024))):
        ref[:, mine] = (y_keep[:, cut] + y_in[0, :, cut].astype(F32)) * scale
    arrived(y_in.at[1], y_recv.at[1])
    arrived(y_in.at[2], y_recv.at[2])
    for ref, cut in ((cor_ref, slice(0, 512)), (ham_ref, slice(512, 1024))):
        ref[:, other] = (y_in[1, :, cut].astype(F32) + y_in[2, :, cut].astype(F32)) * scale

    for copy in started:
        copy.wait_send()
    for dy in range(2):
        for dz in range(4):
            @pl.when((q + dz) % 4 != x)
            def _(dy=dy, dz=dz):
                x_copy(dy, dz).wait_send()


def per_device(o_rows, o_cols, grad_energy, energy):
    total = energy.shape[0] * lax.axis_size("walker")
    dma = pltpu.SemaphoreType.DMA
    out = jax.ShapeDtypeStruct((64, 1024), F32)
    hbm = pl.BlockSpec(memory_space=pl.ANY)
    vmem = pl.BlockSpec(memory_space=pltpu.VMEM)
    return pl.pallas_call(
        functools.partial(kernel, total),
        out_shape=(out, out),
        in_specs=[hbm] * 4,
        out_specs=(vmem, vmem),
        scratch_shapes=[
            pltpu.VMEM((8, 2048, 256), BF16),
            pltpu.VMEM((2048, 512), BF16),
            pltpu.VMEM((2048, 512), BF16),
            pltpu.VMEM((16, 128), F32),
            pltpu.VMEM((2048, 1024), BF16),
            pltpu.VMEM((2, 256, 1024), F32),
            pltpu.VMEM((5, 8, 768), F32),
            pltpu.VMEM((3, 8, 768), F32),
            pltpu.VMEM((4, 2, 8, 256), F32),
            pltpu.VMEM((8, 128, 1024), BF16),
            pltpu.VMEM((8, 128, 1024), BF16),
            pltpu.VMEM((8, 128, 1024), BF16),
            pltpu.VMEM((2, 3, 128, 1024), BF16),
            pltpu.VMEM((2, 128, 1024), F32),
            pltpu.VMEM((3, 64, 1024), BF16),
            pltpu.VMEM((3, 64, 1024), BF16),
            pltpu.VMEM((64, 1024), F32),
            dma((4,)),
            dma((28,)), dma((8, 4)),
            dma((5,)), dma((5,)),
            dma((4,)), dma((4,)),
            dma((8,)), dma((8,)),
            dma((8,)), dma((2, 3)),
            dma((3,)), dma((3,)),
        ],
        compiler_params=pltpu.CompilerParams(
            collective_id=0, has_side_effects=True, vmem_limit_bytes=56 * 1024 * 1024),
    )(o_rows, o_cols, grad_energy, energy.reshape(16, 128))


def solution(mesh):
    in_specs = (
        P("walker", ("prow", "pcol")),
        P("walker", ("pcol", "prow")),
        P("walker", ("pcol", "prow")),
        P("walker"),
    )
    out_specs = (P(("prow", "walker"), "pcol"), P(("prow", "walker"), "pcol"))
    return jax.shard_map(
        per_device, mesh=mesh, in_specs=in_specs, out_specs=out_specs, check_vma=False
    )
```

time: 315 us -> 90.1 us (0.29)
  waiting for transfers between devices: 240 us -> 0 us
  Pallas kernels: 0 us -> 85.9 us
  blocking collectives: 31.3 us -> 0 us
  matrix products: 15.2 us -> 0 us
  between operations: 13.8 us -> 0.64 us
  other arithmetic: 12.2 us -> 0 us
  local copies, waits for them, and re-layouts: 0.01 us -> 3.34 us
    all_gather x3 -> x0, waiting for transfers between devices: 138 us -> none  [the longest x1 61.9 us: per_device(): lax.all_gather(col_shard, 'prow', axis=1, tiled=True)]
    reduce_scatter x1 -> x0, waiting for transfers between devices: 102 us -> none  [per_device(): lax.psum_scatter(tile_product(row_tile, paired), 'walker', scatter_dimens...]
    pallas_call x0 -> x1, Pallas kernels: none -> 85.9 us  [per_device(): pl.pallas_call(functools.partial(kernel, total), out_shape=(out, out), in...]
    psum x1 -> x0, blocking collectives: 31.3 us -> none  [per_device(): lax.psum((column_sums(o_rows), column_sums(o_cols)), 'walker')]
    dot_general x1 -> x0, matrix products: 15.2 us -> none  [tile_product(): lax.dot_general(row_tile, right_tile, (((0,), (0,)), ((), ())), preferred...]
    convert_element_type x3 -> x0, other arithmetic: 8.42 us -> none  [the longest x1 5.44 us: per_device(): weighted = (energy[:, None] * col_tile + grad_tile).astype(jnp.bfloat16)]
    unnamed x6 -> x2, local copies, waits for them, and re-layouts: 0.01 us -> 3.34 us
  transfers between devices with their start and end apart: 4 -> 0, of which waited for: 4 -> 0; matrix products, arithmetic and copies ran while one was open for 3% -> 0% of each run, Pallas kernels for 0% -> 0%
where the time goes in v1:
time: 90.1 us; the launch traced here: 89.9 us
  Pallas kernels  85.9 us (95%)
  local copies, waits for them, and re-layouts  3.34 us (4%)
    pallas_call x1, Pallas kernels, per_device(): pl.pallas_call(functools.partial(kernel, total), out_shape=(out, out), in...  85.9 us
    unnamed x2, local copies, waits for them, and re-layouts  3.34 us

profile of v1, /device:TPU:4, one launch (start us, length us, event | category | flops | bytes accessed | tf_op | source)
XLA Modules:
  0.0 89.9 jit_solution(13357208052795702384)
XLA Ops:
  0.6 85.9 %shard_map.59 = (f32[64,1024]{1,0:T(8,128)}, f32[64,1024]{1,0:T(8,128)}) custom-call(bf16[2048,256]{1,0:T(8,128)(2,1)} %o_hbm.1, bf16[2048,512]{1,0:T(8,128)(2,1)} %c_hbm.1, bf16[2048,512]{1,0:T(8,128)(2,1)} %g_hbm.1, f32[16,128]{1,0:T(8,128)} %bitcast.1), custom_call_target="tpu_custom_call" | custom-call | tf_op jit(solution)/shard_map/pallas_call | solution.py:311
  86.6 1.7 %copy.8 = f32[64,1024]{1,0:T(8,128)} copy(f32[64,1024]{1,0:T(8,128)} %get-tuple-element.4) | data formatting | bytes 524288
  88.3 1.7 %copy.9 = f32[64,1024]{1,0:T(8,128)} copy(f32[64,1024]{1,0:T(8,128)} %get-tuple-element.5) | data formatting | bytes 524288
